TPU v7x, 256 devices: a whole 4x4x8 slice. The times are simulated.
256 devices in a mesh: prow: 32 (over x, z), pcol: 8 (over y, core).
Axes of the slice: x: 4, y: 4, z: 8, core: 2. Of those that a mesh axis runs over, the one named last changes fastest.
Arguments:
- anc_inverse: bfloat16 [4, 32, 256, 16, 8, 256], P(None, 'prow', None, None, 'pcol'), may hold values from -6 to 6
- first_lower: bfloat16 [4, 32, 256, 256], P(None, 'prow', 'pcol'), may hold values from -0.046875 to 0.046875
- second_lower: bfloat16 [4, 32, 256, 256], P(None, 'prow', 'pcol'), may hold values from -0.0546875 to 0.0546875
- second_top: bfloat16 [256, 256], replicated, may hold values from -0.3125 to 0.3125
- struct_first: int32 [128], replicated, may hold values from 0 to 1
- struct_keep: int32 [128], replicated, may hold values from 0 to 1
- pivot_h: float32 [2, 256, 256], replicated, as said below
- pivot_s: float32 [2, 256, 256], replicated, as said below
- shifts: float32 [40], replicated, may hold values from 0.5 to 4
- pole_index: int32 [40], replicated, may hold values from 0 to 39, each once
Outputs:
- first_column: bfloat16 [4, 32, 256, 256], P(None, 'prow', 'pcol')
- first_diag: float32 [256, 256], replicated
- link_column: bfloat16 [256, 256], replicated
- second_column: bfloat16 [4, 32, 256, 256], P(None, 'prow', 'pcol')
- second_diag: float32 [256, 256], replicated
Inputs may be any that keep to these rules, and one draw needn't show every extreme that they name: `struct_first`: 1 marks a block row of the first supernode's structure. `struct_keep`: 1 marks a structure block that the second supernode keeps. `pole_index`: each pole appears once. `pivot_h`: symmetric, with a positive diagonal larger than each row's off-diagonal magnitudes together. `pivot_s`: symmetric, with a positive diagonal larger than each row's off-diagonal magnitudes together.
All inputs are finite; a program needn't handle non-finite values.
Results may differ from a plain program's by a relative error of at most 0.0041.
The roundings to bfloat16 on the way count: a program that leaves them out, or rounds other values in their place, can miss the bound.
Values may be sent and summed in bfloat16 or wider, within the bound.
A program may use at most 64 MiB of HBM per device.

v0:
```python
import jax
import jax.numpy as jnp
from jax import lax
from jax.sharding import PartitionSpec as P


def pivot_inverse(h_block, s_block, shift):
    factor = jnp.linalg.cholesky(h_block + shift * s_block)
    identity = jnp.eye(h_block.shape[0], dtype=jnp.float32)
    return jax.scipy.linalg.cho_solve((factor, True), identity)


def local_mask(flags, row_blocks, grid_rows, my_row):
    table = flags.reshape(row_blocks, grid_rows).astype(jnp.float32)
    return lax.dynamic_index_in_dim(table, my_row, axis=1, keepdims=False)


def per_device(
    anc_inverse,
    first_lower,
    second_lower,
    second_top,
    struct_first,
    struct_keep,
    pivot_h,
    pivot_s,
    shifts,
    pole_index,
):
    grid_rows = lax.axis_size("prow")
    grid_cols = lax.axis_size("pcol")
    my_row = lax.axis_index("prow")
    my_col = lax.axis_index("pcol")
    row_blocks = first_lower.shape[0]
    slab = first_lower.shape[2]
    width = first_lower.shape[3]
    col_blocks = anc_inverse.shape[3]
    first_mask = local_mask(struct_first, row_blocks, grid_rows, my_row)
    second_mask = first_mask * local_mask(struct_keep, row_blocks, grid_rows, my_row)
    lower_first = first_lower[:, 0] * first_mask.astype(jnp.bfloat16)[:, None, None]
    lower_second = second_lower[:, 0] * second_mask.astype(jnp.bfloat16)[:, None, None]
    stacked = jnp.concatenate([lower_first, lower_second], axis=2)[:, None]
    gathered = lax.all_gather(stacked, "prow", axis=1, tiled=True)
    grouped = gathered.reshape(row_blocks, grid_rows // grid_cols, grid_cols, slab, 2 * width)
    columns = lax.all_to_all(grouped, "pcol", split_axis=2, concat_axis=3, tiled=True)
    column_blocks = columns.reshape(col_blocks, width, 2 * width)
    inverse_rows = anc_inverse.reshape(row_blocks, width, col_blocks, width)
    totals = lax.psum(
        jnp.einsum(
            "axcy,cyz->xaz", inverse_rows, column_blocks, preferred_element_type=jnp.float32
        ),
        "pcol",
    )
    row_part = lax.dynamic_slice_in_dim(totals, my_col * slab, slab, 0)
    first_col = (-row_part[:, :, :width] * first_mask[None, :, None]).astype(jnp.bfloat16)
    bridge = jnp.einsum("raw,wz->raz", first_col, second_top, preferred_element_type=jnp.float32)
    second_col = (-(row_part[:, :, width:] + bridge) * second_mask[None, :, None]).astype(
        jnp.bfloat16
    )
    first_rows = lower_first.transpose(1, 0, 2)
    second_rows = lower_second.transpose(1, 0, 2)
    first_term = jnp.einsum(
        "ray,raz->yz", first_rows, first_col, preferred_element_type=jnp.float32
    )
    cross_term = jnp.einsum(
        "ray,raz->yz", first_col, second_rows, preferred_element_type=jnp.float32
    )
    second_term = jnp.einsum(
        "ray,raz->yz", second_rows, second_col, preferred_element_type=jnp.float32
    )
    first_sum, cross_sum, second_sum = lax.psum(
        (first_term, cross_term, second_term), ("prow", "pcol")
    )
    poles = jnp.arange(shifts.shape[0], dtype=jnp.int32)
    shift = jnp.sum(jnp.where(poles == pole_index[0], shifts, 0.0))
    first_diag = pivot_inverse(pivot_h[0], pivot_s[0], shift) - first_sum
    link_col = (
        -(
            cross_sum
            + jnp.dot(
                first_diag.astype(jnp.bfloat16), second_top, preferred_element_type=jnp.float32
            )
        )
    ).astype(jnp.bfloat16)
    second_diag = (
        pivot_inverse(pivot_h[1], pivot_s[1], shift)
        - second_sum
        - jnp.einsum("yz,yw->zw", second_top, link_col, preferred_element_type=jnp.float32)
    )
    return (
        first_col.transpose(1, 0, 2)[:, None],
        first_diag,
        link_col,
        second_col.transpose(1, 0, 2)[:, None],
        second_diag,
    )


def solution(mesh):
    return jax.shard_map(
        per_device,
        mesh=mesh,
        in_specs=(
            P(None, "prow", None, None, "pcol", None),
            P(None, "prow", "pcol", None),
            P(None, "prow", "pcol", None),
            P(),
            P(),
            P(),
            P(),
            P(),
            P(),
            P(),
        ),
        out_specs=(P(None, "prow", "pcol", None), P(), P(), P(None, "prow", "pcol", None), P()),
        check_vma=False,
    )
```

profile of v0, /device:TPU:8, one launch (start us, length us, event | category | flops | bytes accessed | tf_op | source)
XLA Modules:
  0.0 544.1 jit_solution(14048645056738182097)
XLA Ops:
  9.0 0.9 bitcast_multiply_fusion
  11.5 1.1 fusion.48
  12.7 1.1 fusion.47
  13.9 1.9 fusion.43
  18.5 11.7 %cholesky.130 = f32[128,128]{1,0:T(8,128)S(1)} custom-call(f32[128,128]{1,0:T(8,128)S(1)} %cholesky.194), custom_call_target="Cholesky" | custom-call | tf_op jit(solution)/shard_map/jit(cholesky)/cholesky | solution.py:8
  30.3 9.8 %custom-call.15 = f32[1,128,128]{1,2,0:T(8,128)S(1)} custom-call(f32[1,128,128]{2,1,0:T(8,128)S(1)} %get-tuple-element.84), custom_call_target="InvertDiagBlocksLowerTriangular" | custom-call | tf_op jit(solution)/shard_map/jit(cholesky)/cholesky | solution.py:8
  40.6 11.7 %cholesky.147 = f32[128,128]{1,0:T(8,128)S(1)} custom-call(f32[128,128]{1,0:T(8,128)S(1)} %convolution_subtract_fusion.5), custom_call_target="Cholesky" | custom-call | tf_op jit(solution)/shard_map/jit(cholesky)/cholesky | solution.py:8
  55.0 41.5 %all-gather.3.cloned.1.call-done = bf16[4,1024,512]{2,1,0:T(8,128)(2,1)} async-done(((bf16[4,32,512]{2,1,0:T(8,128)(2,1)}), bf16[4,1024,512]{2,1,0:T(8,128)(2,1)}) %all-gather.3.cloned.1.call-update) | async-done | bytes 4194320 | tf_op jit(solution)/shard_map/all_gather | solution.py:43
  96.5 4.7 copy.82
  101.2 5.2 all-to-all-start
  106.4 4.0 while.4
  107.0 1.4 bitcast_dynamic-update-slice_fusion.4
  109.0 1.4 bitcast_dynamic-update-slice_fusion.4
  110.4 19.7 %custom-call.16 = f32[2,128,128]{1,2,0:T(8,128)S(1)} custom-call(f32[2,128,128]{2,1,0:T(8,128)S(1)} %get-tuple-element.21), custom_call_target="InvertDiagBlocksLowerTriangular" | custom-call | tf_op jit(solution)/shard_map/jit(_cho_solve)/triangular_solve | solution.py:10
  130.1 11.7 %cholesky.164 = f32[128,128]{1,0:T(8,128)S(1)} custom-call(f32[128,128]{1,0:T(8,128)S(1)} %cholesky.197), custom_call_target="Cholesky" | custom-call | tf_op jit(solution)/shard_map/jit(cholesky)/cholesky | solution.py:8
  141.9 9.8 %custom-call.17 = f32[1,128,128]{1,2,0:T(8,128)S(1)} custom-call(f32[1,128,128]{2,1,0:T(8,128)S(1)} %get-tuple-element.80), custom_call_target="InvertDiagBlocksLowerTriangular" | custom-call | tf_op jit(solution)/shard_map/jit(cholesky)/cholesky | solution.py:8
  152.2 11.7 %cholesky.181 = f32[128,128]{1,0:T(8,128)S(1)} custom-call(f32[128,128]{1,0:T(8,128)S(1)} %convolution_subtract_fusion.4), custom_call_target="Cholesky" | custom-call | tf_op jit(solution)/shard_map/jit(cholesky)/cholesky | solution.py:8
  166.6 4.0 while.5
  167.2 1.4 bitcast_dynamic-update-slice_fusion.5
  169.2 1.4 bitcast_dynamic-update-slice_fusion.5
  170.6 19.9 %custom-call.18 = f32[2,128,128]{1,2,0:T(8,128)S(1)} custom-call(f32[2,128,128]{2,1,0:T(8,128)S(1)} %get-tuple-element.22), custom_call_target="InvertDiagBlocksLowerTriangular" | custom-call | tf_op jit(solution)/shard_map/jit(_cho_solve)/triangular_solve | solution.py:10
  192.3 2.5 copy.83
  194.8 9.6 %fusion.2 = f32[256,4,512]{2,0,1:T(8,128)} fusion(bf16[16,256,512,1]{2,1,0,3:T(8,128)(2,1)S(1)} %bitcast.134, bf16[4,256,16,256]{3,2,1,0:T(8,128)(2,1)} %bitcast.136), kind=kOutput, calls=%fused_computation.6 | convolution fusion | flops 4294967296 | bytes 14680064 | tf_op jit(solution)/shard_map/axcy,cyz->xaz/dot_general | solution.py:49
  206.0 64.4 %all-reduce.5.cloned.1.call-done = f32[256,4,512]{2,0,1:T(8,128)} async-done(((f32[256,4,512]{2,0,1:T(8,128)}), f32[256,4,512]{2,0,1:T(8,128)}) %all-reduce.5.cloned.1.call-update) | async-done | bytes 2097168 | tf_op jit(solution)/shard_map/psum | solution.py:48
  270.3 1.0 fusion.15
  273.1 1.1 fusion.10
  274.2 0.9 convolution_bitcast_fusion.1
  275.5 1.6 fusion.71
  277.1 256.3 %all-reduce.7.cloned.1.call-done = (f32[256,256]{1,0:T(8,128)}, f32[256,256]{1,0:T(8,128)}, f32[256,256]{1,0:T(8,128)}) async-done(((f32[256,256]{1,0:T(8,128)}, f32[256,256]{1,0:T(8,128)}, f32[256,256]{1,0:T(8,128)}), (f32[256,256]{1,0:T(8,128)}, f32[256,256]{1,0:T(8,128)}, f32[256,256]{1,0:T(8,128)})) %all-reduce.7.cloned.1.call-update) | async-done | bytes 786448 | tf_op jit(solution)/shard_map/psum | solution.py:71
  533.4 1.0 maximum_subtract_fusion
  534.4 1.2 fusion.7
  535.6 1.9 fusion.6
  (77 shorter events, 17.8 us)
Async XLA Ops:
  7.2 266.0 %copy-start = (bf16[256,256]{1,0:T(8,128)(2,1)S(1)}, bf16[256,256]{1,0:T(8,128)(2,1)}, u32[]{:S(2)}) copy-start(bf16[256,256]{1,0:T(8,128)(2,1)} %param.16) | copy-start | bytes 393220
  7.2 89.3 %all-gather.3.cloned.1.call-start = ((), (), s32[]{:S(2)}) async-start(), calls=%async_computation.2 | async-start | bytes 4325376 | tf_op jit(solution)/shard_map/all_gather | solution.py:43
  101.2 91.1 %all-to-all-start = ((bf16[4,4,8,32,512]{4,3,1,0,2:T(8,128)(2,1)}), bf16[4,4,8,32,512]{4,3,1,0,2:T(8,128)(2,1)}, u32[]{:S(2)}, u32[]{:S(2)}) async-start(bf16[4,4,8,32,512]{4,3,1,0,2:T(8,128)(2,1)} %copy.82), calls=%async_computation | async-start | bytes 8388608 | tf_op jit(solution)/shard_map/all_to_all | solution.py:45
  106.4 164.0 %all-reduce.5.cloned.1.call-start = ((), (), s32[]{:S(2)}) async-start(), calls=%async_computation.1 | async-start | bytes 4194304 | tf_op jit(solution)/shard_map/psum | solution.py:48
  204.4 329.0 %all-reduce.7.cloned.1.call-start = ((), (), s32[]{:S(2)}) async-start(), calls=%async_computation.3 | async-start | bytes 1572864 | tf_op jit(solution)/shard_map/psum | solution.py:71
  274.2 263.3 %copy-start.3 = (bf16[32,4,256]{2,0,1:T(8,128)(2,1)}, bf16[32,4,256]{2,0,1:T(8,128)(2,1)S(1)}, u32[]{:S(2)}) copy-start(bf16[32,4,256]{2,0,1:T(8,128)(2,1)S(1)} %fusion.10) | copy-start | bytes 196612
  534.4 3.2 copy-start.1
  535.6 2.0 copy-start.2
Sparse Core Ops, SparseCore 0:
  11.6 84.8 all-gather.2
  204.5 65.7 all-reduce.4
  276.7 256.6 all-reduce.6
where the time goes:
time: 545 us; the launch traced here: 544 us
  waiting for transfers between devices  362 us (66%)
  other arithmetic  120 us (22%)
  matrix products  20.9 us (4%)
  local copies, waits for them, and re-layouts  18.6 us (3%)
  between operations  16.7 us (3%)
    psum x1, waiting for transfers between devices, per_device(): lax.psum((first_term, cross_term, second_term), ('prow', 'pcol'))  256 us
    another operation x14, other arithmetic, pivot_inverse(): factor = jnp.linalg.cholesky(h_block + shift * s_block)  69.2 us
    psum x1, waiting for transfers between devices, per_device(): lax.psum(jnp.einsum('axcy,cyz->xaz', inverse_rows, column_blocks, preferr...  64.4 us
    all_gather x1, waiting for transfers between devices, per_device(): gathered = lax.all_gather(stacked, 'prow', axis=1, tiled=True)  41.5 us
    another operation x5, other arithmetic, pivot_inverse(): return jax.scipy.linalg.cho_solve((factor, True), identity)  39.6 us
  transfers between devices with their start and end apart: 4, of which 3 were waited for; matrix products, arithmetic and copies ran while one was open for 24% of the time, Pallas kernels for 0%

commit v1 on v0

--- a/solution.py
+++ b/solution.py
@@ -45,11 +45,14 @@
     columns = lax.all_to_all(grouped, "pcol", split_axis=2, concat_axis=3, tiled=True)
     column_blocks = columns.reshape(col_blocks, width, 2 * width)
     inverse_rows = anc_inverse.reshape(row_blocks, width, col_blocks, width)
-    totals = lax.psum(
-        jnp.einsum(
-            "axcy,cyz->xaz", inverse_rows, column_blocks, preferred_element_type=jnp.float32
+    totals = jnp.sum(
+        lax.all_gather(
+            jnp.einsum(
+                "axcy,cyz->xaz", inverse_rows, column_blocks, preferred_element_type=jnp.float32
+            ),
+            "pcol",
         ),
-        "pcol",
+        axis=0,
     )
     row_part = lax.dynamic_slice_in_dim(totals, my_col * slab, slab, 0)
     first_col = (-row_part[:, :, :width] * first_mask[None, :, None]).astype(jnp.bfloat16)

time: 545 us -> 591 us (1.084)
  blocking collectives: 0 us -> 53.8 us
  waiting for transfers between devices: 362 us -> 334 us
  local copies, waits for them, and re-layouts: 18.6 us -> 30.6 us
  other arithmetic: 120 us -> 127 us
    psum x1 -> x0, waiting for transfers between devices: 64.4 us -> none  [per_device(): lax.psum(jnp.einsum('axcy,cyz->xaz', inverse_rows, column_blocks, preferr...]
    all_to_all x0 -> x1, blocking collectives: none -> 53.8 us  [per_device(): lax.all_to_all(grouped, 'pcol', split_axis=2, concat_axis=3, tiled=True)]
    all_gather x1, waiting for transfers between devices: 41.5 us -> 84.7 us  [per_device(): gathered = lax.all_gather(stacked, 'prow', axis=1, tiled=True)]
    unnamed x12 -> x33, local copies, waits for them, and re-layouts: 0.54 us -> 18.2 us
    reduce_sum x0 -> x1, other arithmetic: none -> 8.14 us  [per_device(): jnp.sum(lax.all_gather(jnp.einsum('axcy,cyz->xaz', inverse_rows, column_b...]
    psum x1, waiting for transfers between devices: 256 us -> 249 us  [per_device(): lax.psum((first_term, cross_term, second_term), ('prow', 'pcol'))]
  transfers between devices with their start and end apart: 4 -> 3, of which waited for: 3 -> 2; matrix products, arithmetic and copies ran while one was open for 24% -> 22% of each run, Pallas kernels for 0% -> 0%
where the time goes in v1:
time: 591 us; the launch traced here: 586 us
  waiting for transfers between devices  334 us (57%)
  other arithmetic  127 us (21%)
  blocking collectives  53.8 us (9%)
  local copies, waits for them, and re-layouts  30.6 us (5%)
  matrix products  22.5 us (4%)
  between operations  17.1 us (3%)
    psum x1, waiting for transfers between devices, per_device(): lax.psum((first_term, cross_term, second_term), ('prow', 'pcol'))  249 us
    all_gather x1, waiting for transfers between devices, per_device(): gathered = lax.all_gather(stacked, 'prow', axis=1, tiled=True)  84.7 us
    another operation x14, other arithmetic, pivot_inverse(): factor = jnp.linalg.cholesky(h_block + shift * s_block)  69.2 us
    all_to_all x1, blocking collectives, per_device(): lax.all_to_all(grouped, 'pcol', split_axis=2, concat_axis=3, tiled=True)  53.8 us
    another operation x5, other arithmetic, pivot_inverse(): return jax.scipy.linalg.cho_solve((factor, True), identity)  39.6 us
    unnamed x33, local copies, waits for them, and re-layouts  18.2 us
  transfers between devices with their start and end apart: 3, of which 2 were waited for; matrix products, arithmetic and copies ran while one was open for 22% of the time, Pallas kernels for 0%

profile of v1, /device:TPU:8, one launch (start us, length us, event | category | flops | bytes accessed | tf_op | source)
XLA Modules:
  0.0 585.5 jit_solution(2530771170444857881)
XLA Ops:
  9.9 1.6 bitcast_multiply_fusion.1
  11.5 1.5 pad_maximum_fusion
  13.0 84.7 %all-gather.5.cloned.1.call-done = bf16[4,1024,512]{2,1,0:T(8,128)(2,1)} async-done(((bf16[4,32,512]{2,1,0:T(8,128)(2,1)}), bf16[4,1024,512]{2,1,0:T(8,128)(2,1)}) %all-gather.5.cloned.1.call-update) | async-done | bytes 4194320 | tf_op jit(solution)/shard_map/all_gather | solution.py:43
  97.8 2.7 copy.50
  100.5 53.8 %all_to_all.4 = bf16[4,4,8,32,512]{4,3,1,0,2:T(8,128)(2,1)S(1)} all-to-all(bf16[4,4,8,32,512]{4,3,1,0,2:T(8,128)(2,1)S(1)} %copy.50), channel_id=1, replica_groups=mesh['prow'=32,'pcol'=8] {'pcol'}, dimensions={2} | all-to-all | bytes 8388608 | tf_op jit(solution)/shard_map/all_to_all | solution.py:45
  154.8 1.6 slice-done.1
  156.4 7.2 %fusion.2 = f32[256,4,512]{0,2,1:T(8,128)} fusion(bf16[16,256,512,1]{2,1,0,3:T(8,128)(2,1)S(1)} %bitcast.143, bf16[4,256,16,256]{3,2,1,0:T(8,128)(2,1)S(1)} %bitcast.147), kind=kOutput, calls=%fused_computation.6 | convolution fusion | flops 4294967296 | bytes 14680064 | tf_op jit(solution)/shard_map/axcy,cyz->xaz/dot_general | solution.py:50
  167.9 11.7 %cholesky.130 = f32[128,128]{1,0:T(8,128)S(1)} custom-call(f32[128,128]{1,0:T(8,128)S(1)} %cholesky.194), custom_call_target="Cholesky" | custom-call | tf_op jit(solution)/shard_map/jit(cholesky)/cholesky | solution.py:8
  179.7 9.8 %custom-call.15 = f32[1,128,128]{1,2,0:T(8,128)S(1)} custom-call(f32[1,128,128]{2,1,0:T(8,128)S(1)} %get-tuple-element.81), custom_call_target="InvertDiagBlocksLowerTriangular" | custom-call | tf_op jit(solution)/shard_map/jit(cholesky)/cholesky | solution.py:8
  190.0 11.7 %cholesky.147 = f32[128,128]{1,0:T(8,128)S(1)} custom-call(f32[128,128]{1,0:T(8,128)S(1)} %convolution_subtract_fusion.5), custom_call_target="Cholesky" | custom-call | tf_op jit(solution)/shard_map/jit(cholesky)/cholesky | solution.py:8
  204.4 4.2 while.4
  205.2 1.4 bitcast_dynamic-update-slice_fusion.4
  207.2 1.4 bitcast_dynamic-update-slice_fusion.4
  208.6 19.7 %custom-call.16 = f32[2,128,128]{1,2,0:T(8,128)S(1)} custom-call(f32[2,128,128]{2,1,0:T(8,128)S(1)} %get-tuple-element.21), custom_call_target="InvertDiagBlocksLowerTriangular" | custom-call | tf_op jit(solution)/shard_map/jit(_cho_solve)/triangular_solve | solution.py:10
  228.3 11.7 %cholesky.164 = f32[128,128]{1,0:T(8,128)S(1)} custom-call(f32[128,128]{1,0:T(8,128)S(1)} %cholesky.197), custom_call_target="Cholesky" | custom-call | tf_op jit(solution)/shard_map/jit(cholesky)/cholesky | solution.py:8
  240.1 9.8 %custom-call.17 = f32[1,128,128]{1,2,0:T(8,128)S(1)} custom-call(f32[1,128,128]{2,1,0:T(8,128)S(1)} %get-tuple-element.77), custom_call_target="InvertDiagBlocksLowerTriangular" | custom-call | tf_op jit(solution)/shard_map/jit(cholesky)/cholesky | solution.py:8
  250.4 11.7 %cholesky.181 = f32[128,128]{1,0:T(8,128)S(1)} custom-call(f32[128,128]{1,0:T(8,128)S(1)} %convolution_subtract_fusion.4), custom_call_target="Cholesky" | custom-call | tf_op jit(solution)/shard_map/jit(cholesky)/cholesky | solution.py:8
  264.8 4.0 while.5
  265.4 1.4 bitcast_dynamic-update-slice_fusion.5
  267.4 1.4 bitcast_dynamic-update-slice_fusion.5
  268.8 19.9 %custom-call.18 = f32[2,128,128]{1,2,0:T(8,128)S(1)} custom-call(f32[2,128,128]{2,1,0:T(8,128)S(1)} %get-tuple-element.22), custom_call_target="InvertDiagBlocksLowerTriangular" | custom-call | tf_op jit(solution)/shard_map/jit(_cho_solve)/triangular_solve | solution.py:10
  292.3 1.0 convolution_subtract_fusion
  293.3 15.7 %copy.75 = f32[256,8,8,256]{3,2,1,0:T(8,128)} copy(f32[256,8,8,256]{3,1,2,0:T(8,128)} %bitcast.141) | data formatting | bytes 33554432
  309.0 8.1 %reduce_sum.18 = f32[256,4,512]{0,2,1:T(8,128)S(1)} reduce(f32[8,256,4,512]{1,0,3,2:T(8,128)} %bitcast.140, f32[]{:T(128)} %constant.84.clone.1), dimensions={0}, to_apply=%region_0.1 | reduce | flops 3670016 | bytes 18874372 | tf_op jit(solution)/shard_map/reduce_sum | solution.py:48
  317.7 1.8 convolution_bitcast_fusion.3
  319.5 1.8 convolution_bitcast_fusion.2
  321.6 1.8 convolution_bitcast_fusion.1
  323.4 1.2 fusion.34
  325.3 249.2 %all-reduce.4.cloned.1.call-done = (f32[256,256]{1,0:T(8,128)}, f32[256,256]{1,0:T(8,128)}, f32[256,256]{1,0:T(8,128)}) async-done(((f32[256,256]{1,0:T(8,128)}, f32[256,256]{1,0:T(8,128)}, f32[256,256]{1,0:T(8,128)}), (f32[256,256]{1,0:T(8,128)}, f32[256,256]{1,0:T(8,128)}, f32[256,256]{1,0:T(8,128)})) %all-reduce.4.cloned.1.call-update) | async-done | bytes 786448 | tf_op jit(solution)/shard_map/psum | solution.py:74
  574.6 1.0 maximum_subtract_fusion
  575.5 1.2 fusion.7
  576.8 1.9 fusion.6
  (100 shorter events, 18.9 us)
Async XLA Ops:
  7.2 314.2 %copy-start = (bf16[256,256]{1,0:T(8,128)(2,1)S(1)}, bf16[256,256]{1,0:T(8,128)(2,1)}, u32[]{:S(2)}) copy-start(bf16[256,256]{1,0:T(8,128)(2,1)} %param.16) | copy-start | bytes 393220
  7.2 90.6 %all-gather.5.cloned.1.call-start = ((), (), s32[]{:S(2)}) async-start(), calls=%async_computation.1 | async-start | bytes 4325376 | tf_op jit(solution)/shard_map/all_gather | solution.py:43
  9.9 1.6 copy-start.2
  13.0 280.3 %all-gather.7.cloned.1.call-start = ((), (), s32[]{:S(2)}) async-start(), calls=%async_computation.2 | async-start | bytes 18874368 | tf_op jit(solution)/shard_map/all_gather | solution.py:49
  100.4 54.4 %slice-start = ((s8[8388608]{0:T(1024)(128)(4,1)}), s8[4194304]{0:T(1024)(128)(4,1)S(1)}, s32[]{:S(2)}) async-start(s8[8388608]{0:T(1024)(128)(4,1)} %bitcast.145), calls=%async_computation.4 | async-start | bytes 8388608
  154.2 2.2 slice-start.1
  156.4 7.8 %copy-start.4 = (f32[2,256,256]{2,1,0:T(8,128)S(1)}, f32[2,256,256]{2,1,0:T(8,128)}, u32[]{:S(2)}) copy-start(f32[2,256,256]{2,1,0:T(8,128)} %param.19) | copy-start | bytes 1572868
  156.4 8.0 %copy-start.5 = (f32[2,256,256]{2,1,0:T(8,128)S(1)}, f32[2,256,256]{2,1,0:T(8,128)}, u32[]{:S(2)}) copy-start(f32[2,256,256]{2,1,0:T(8,128)} %param.20) | copy-start | bytes 1572868
  163.6 0.9 copy-start.9
  163.6 0.9 copy-start.10
  163.7 410.9 %all-reduce.4.cloned.1.call-start = ((), (), s32[]{:S(2)}) async-start(), calls=%async_computation.3 | async-start | bytes 1572864 | tf_op jit(solution)/shard_map/psum | solution.py:74
  288.7 20.3 %copy-start.3 = (f32[2,128,128]{1,2,0:T(8,128)}, f32[2,128,128]{1,2,0:T(8,128)S(1)}, u32[]{:S(2)}) copy-start(f32[2,128,128]{1,2,0:T(8,128)S(1)} %custom-call.18) | copy-start | bytes 393220
  317.5 257.1 %copy-start.6 = (f32[128,256]{1,0:T(8,128)S(1)}, f32[128,256]{1,0:T(8,128)}, u32[]{:S(2)}) copy-start(f32[128,256]{1,0:T(8,128)} %fusion.31) | copy-start | bytes 393220
  321.6 257.1 %copy-start.8 = (bf16[32,4,256]{2,0,1:T(8,128)(2,1)}, bf16[32,4,256]{2,0,1:T(8,128)(2,1)S(1)}, u32[]{:S(2)}) copy-start(bf16[32,4,256]{2,0,1:T(8,128)(2,1)S(1)} %fusion.10) | copy-start | bytes 196612
  575.5 3.2 copy-start.1
  576.8 2.0 copy-start.7
Sparse Core Ops, SparseCore 0:
  13.1 84.6 all-gather.4
  163.8 83.5 all-gather.6
  323.5 250.9 all-reduce.3
